TPU v7x, 256 devices: a whole 4x4x8 slice. The times are simulated.
256 devices in a mesh: wide: 32 (over z, x), narrow: 8 (over y, core).
Axes of the slice: x: 4, y: 4, z: 8, core: 2. Of those that a mesh axis runs over, the one named last changes fastest.
Arguments:
- cube: bfloat16 [256, 1536, 224], P('narrow', 'wide')
Outputs:
- restored: bfloat16 [256, 1536, 224], P('narrow', 'wide')
- projector: float32 [224, 224], replicated
All inputs are finite; a program needn't handle non-finite values.
Results may differ from a plain program's by a relative error of at most 0.0034.
Values may be sent and summed in bfloat16 or wider, within the bound.
A program may use at most 64 MiB of HBM per device.

v0:
```python
import jax
import jax.numpy as jnp
from jax import lax
from jax.sharding import PartitionSpec as P

TILE_ROWS = 32
TILE_COLS = 48
BANDS = 224
RANK = 16
POWER_ITERS = 4
TV_ITERS = 3


hi_prec = lax.Precision.HIGHEST


def with_halo(cells, sides, width):
    for axis, dim in sides:
        count = lax.axis_size(axis)
        ends = count - 1
        head = lax.slice_in_dim(cells, 0, width, axis=dim)
        tail = lax.slice_in_dim(cells, cells.shape[dim] - width, cells.shape[dim], axis=dim)
        cells = jnp.concatenate(
            [
                lax.ppermute(tail, axis, [(i, (i + 1) % count) for i in range(ends)]),
                cells,
                lax.ppermute(head, axis, [((i + 1) % count, i) for i in range(ends)]),
            ],
            axis=dim,
        )
    return cells


def smooth_step(field, fitted, grow, gcol, height, width):
    mask_x = ((grow >= 0) & (grow + 1 < height)).astype(jnp.float32)
    mask_y = ((gcol >= 0) & (gcol + 1 < width)).astype(jnp.float32)
    corner = field[:-1, :-1]
    grad_x = (field[1:, :-1] - corner) * mask_x[:-1, None, None]
    grad_y = (field[:-1, 1:] - corner) * mask_y[None, :-1, None]
    magnitude = jnp.sqrt(grad_x * grad_x + grad_y * grad_y + 0.25)
    flow_x = grad_x / magnitude
    flow_y = grad_y / magnitude
    diverg = flow_x[1:, 1:] - flow_x[:-1, 1:] + flow_y[1:, 1:] - flow_y[1:, :-1]
    centre = field[1:-1, 1:-1]
    return centre - 0.5 * (centre - fitted[1:-1, 1:-1] - 0.5 * diverg)


def subspace(gram):
    bands = lax.broadcasted_iota(jnp.float32, (BANDS, RANK), 0)
    cols = lax.broadcasted_iota(jnp.float32, (BANDS, RANK), 1)
    basis = jnp.cos(jnp.pi * (bands + 0.5) * cols / BANDS)
    for step in range(POWER_ITERS):
        grown = jnp.dot(gram, basis, precision=hi_prec)
        inner = jnp.dot(grown.T, grown, precision=hi_prec)
        lower = jnp.linalg.cholesky(inner)
        basis = jax.scipy.linalg.solve_triangular(lower, grown.T, lower=True).T
    return basis


def project_tile(block, basis, basis_low):
    loading = jnp.einsum("hwb,br->hwr", block, basis_low, preferred_element_type=jnp.float32)
    return jnp.einsum("hwr,br->hwb", loading, basis, precision=hi_prec)


def body(cube):
    n_rows = lax.axis_size("narrow")
    n_cols = lax.axis_size("wide")
    height = TILE_ROWS * n_rows
    width = TILE_COLS * n_cols
    row_base = lax.axis_index("narrow") * TILE_ROWS
    col_base = lax.axis_index("wide") * TILE_COLS
    flat = cube.reshape(TILE_ROWS * TILE_COLS, BANDS)
    local = lax.dot_general(
        flat, flat, (((0,), (0,)), ((), ())), preferred_element_type=jnp.float32
    )
    total = lax.psum(local, ("wide", "narrow"))
    gram = total / (height * width)
    basis = subspace(gram)
    projector = jnp.dot(basis, basis.T, precision=hi_prec)
    basis_low = basis.astype(jnp.bfloat16)
    fitted = project_tile(cube, basis, basis_low)
    fitted_pad = jnp.pad(fitted, ((1, 1), (1, 1), (0, 0)))
    rows = row_base - 1 + jnp.arange(TILE_ROWS + 2, dtype=jnp.int32)
    cols = col_base - 1 + jnp.arange(TILE_COLS + 2, dtype=jnp.int32)
    field = fitted
    for step in range(TV_ITERS):
        field_ext = with_halo(field, (("narrow", 0), ("wide", 1)), 1)
        field = smooth_step(field_ext, fitted_pad, rows, cols, height, width)
    return (field.astype(jnp.bfloat16), projector)


def solution(mesh):
    return jax.shard_map(
        body,
        mesh=mesh,
        in_specs=(P("narrow", "wide", None),),
        out_specs=(P("narrow", "wide", None), P()),
        check_vma=False,
    )
```

profile of v0, /device:TPU:1, one launch (start us, length us, event | category | flops | bytes accessed | tf_op | source)
XLA Modules:
  0.0 362.7 jit_solution(9770431130495249108)
XLA Ops:
  9.5 260.3 %all-reduce.2.cloned.1.call-done = f32[224,224]{1,0:T(8,128)} async-done(((f32[224,224]{1,0:T(8,128)}), f32[224,224]{1,0:T(8,128)}) %all-reduce.2.cloned.1.call-update) | async-done | bytes 200720 | tf_op jit(solution)/shard_map/psum | solution.py:76
  269.8 1.7 fusion.34
  271.7 1.5 cholesky.74
  274.5 1.2 custom-call.8
  277.4 1.5 cholesky.85
  280.2 1.2 custom-call.9
  283.1 1.5 cholesky.96
  285.9 1.2 custom-call.10
  288.9 1.5 cholesky.107
  293.6 1.5 fusion.46
  295.1 4.7 %collective-permute-start = (f32[1,48,224]{2,1,0:T(8,128)S(1)}, f32[1,48,224]{2,1,0:T(8,128)S(1)}, u32[]{:S(2)}, u32[]{:S(2)}) collective-permute-start(f32[1,48,224]{2,1,0:T(8,128)S(1)} %get-tuple-element.20), channel_id=1, source_target_pairs={{0,1},{1,2},{2,3},{3,4},{4,5},{5,6},{6,7},{8,9},{9,10},{10,11},{11... | collective-permute-start | bytes 129032 | tf_op jit(solution)/shard_map/ppermute | solution.py:25
  299.8 1.9 collective-permute-start.1
  301.8 3.5 collective-permute-done.1
  305.3 2.9 collective-permute-start.2
  308.2 1.3 collective-permute-start.3
  309.8 3.2 collective-permute-done.3
  312.9 1.4 fusion.14
  315.0 3.3 collective-permute-start.4
  318.3 1.9 collective-permute-start.5
  320.3 3.5 collective-permute-done.5
  323.8 3.5 collective-permute-start.6
  327.3 1.3 collective-permute-start.7
  328.8 3.2 collective-permute-done.7
  331.9 1.4 fusion.12
  334.4 3.5 collective-permute-start.8
  338.0 1.9 collective-permute-start.9
  339.9 3.5 collective-permute-done.9
  343.5 3.0 collective-permute-start.10
  347.5 1.5 collective-permute-start.11
  349.2 3.2 collective-permute-done.11
  352.4 1.4 fusion.10
  353.8 2.0 fusion.19
  (61 shorter events, 18.4 us)
Async XLA Ops:
  7.2 1.1 copy-start
  7.2 262.6 %all-reduce.2.cloned.1.call-start = ((), (), s32[]{:S(2)}) async-start(), calls=%async_computation | async-start | bytes 458752 | tf_op jit(solution)/shard_map/psum | solution.py:76
  295.1 6.7 %collective-permute-start = (f32[1,48,224]{2,1,0:T(8,128)S(1)}, f32[1,48,224]{2,1,0:T(8,128)S(1)}, u32[]{:S(2)}, u32[]{:S(2)}) collective-permute-start(f32[1,48,224]{2,1,0:T(8,128)S(1)} %get-tuple-element.20), channel_id=1, source_target_pairs={{0,1},{1,2},{2,3},{3,4},{4,5},{5,6},{6,7},{8,9},{9,10},{10,11},{11... | collective-permute-start | bytes 129032 | tf_op jit(solution)/shard_map/ppermute | solution.py:25
  299.8 5.4 %collective-permute-start.1 = (f32[1,48,224]{2,1,0:T(8,128)S(1)}, f32[1,48,224]{2,1,0:T(8,128)S(1)}, u32[]{:S(2)}, u32[]{:S(2)}) collective-permute-start(f32[1,48,224]{2,1,0:T(8,128)S(1)} %get-tuple-element.21), channel_id=1, source_target_pairs={{1,0},{2,1},{3,2},{4,3},{5,4},{6,5},{7,6},{9,8},{10,9},{11,10},{12... | collective-permute-start | bytes 129032 | tf_op jit(solution)/shard_map/ppermute | solution.py:27
  305.3 4.3 %collective-permute-start.2 = (f32[34,1,224]{2,1,0:T(1,128)S(1)}, f32[34,1,224]{2,1,0:T(1,128)S(1)}, u32[]{:S(2)}, u32[]{:S(2)}) collective-permute-start(f32[34,1,224]{2,1,0:T(1,128)S(1)} %get-tuple-element.15), channel_id=1, source_target_pairs={{0,8},{8,16},{16,24},{24,32},{32,40},{40,48},{48,56},{56,64},{64,7... | collective-permute-start | bytes 91400 | tf_op jit(solution)/shard_map/ppermute | solution.py:25
  308.2 4.7 %collective-permute-start.3 = (f32[34,1,224]{2,1,0:T(1,128)S(1)}, f32[34,1,224]{2,1,0:T(1,128)S(1)}, u32[]{:S(2)}, u32[]{:S(2)}) collective-permute-start(f32[34,1,224]{2,1,0:T(1,128)S(1)} %get-tuple-element.14), channel_id=1, source_target_pairs={{8,0},{16,8},{24,16},{32,24},{40,32},{48,40},{56,48},{64,56},{72,6... | collective-permute-start | bytes 91400 | tf_op jit(solution)/shard_map/ppermute | solution.py:27
  315.0 5.3 %collective-permute-start.4 = (f32[1,48,224]{2,1,0:T(8,128)S(1)}, f32[1,48,224]{2,1,0:T(8,128)S(1)}, u32[]{:S(2)}, u32[]{:S(2)}) collective-permute-start(f32[1,48,224]{2,1,0:T(8,128)S(1)} %get-tuple-element.18), channel_id=1, source_target_pairs={{0,1},{1,2},{2,3},{3,4},{4,5},{5,6},{6,7},{8,9},{9,10},{10,11},{11... | collective-permute-start | bytes 129032 | tf_op jit(solution)/shard_map/ppermute | solution.py:25
  318.3 5.4 %collective-permute-start.5 = (f32[1,48,224]{2,1,0:T(8,128)S(1)}, f32[1,48,224]{2,1,0:T(8,128)S(1)}, u32[]{:S(2)}, u32[]{:S(2)}) collective-permute-start(f32[1,48,224]{2,1,0:T(8,128)S(1)} %get-tuple-element.19), channel_id=1, source_target_pairs={{1,0},{2,1},{3,2},{4,3},{5,4},{6,5},{7,6},{9,8},{10,9},{11,10},{12... | collective-permute-start | bytes 129032 | tf_op jit(solution)/shard_map/ppermute | solution.py:27
  323.8 4.8 %collective-permute-start.6 = (f32[34,1,224]{2,1,0:T(1,128)S(1)}, f32[34,1,224]{2,1,0:T(1,128)S(1)}, u32[]{:S(2)}, u32[]{:S(2)}) collective-permute-start(f32[34,1,224]{2,1,0:T(1,128)S(1)} %get-tuple-element.13), channel_id=1, source_target_pairs={{0,8},{8,16},{16,24},{24,32},{32,40},{40,48},{48,56},{56,64},{64,7... | collective-permute-start | bytes 91400 | tf_op jit(solution)/shard_map/ppermute | solution.py:25
  327.3 4.7 %collective-permute-start.7 = (f32[34,1,224]{2,1,0:T(1,128)S(1)}, f32[34,1,224]{2,1,0:T(1,128)S(1)}, u32[]{:S(2)}, u32[]{:S(2)}) collective-permute-start(f32[34,1,224]{2,1,0:T(1,128)S(1)} %get-tuple-element.12), channel_id=1, source_target_pairs={{8,0},{16,8},{24,16},{32,24},{40,32},{48,40},{56,48},{64,56},{72,6... | collective-permute-start | bytes 91400 | tf_op jit(solution)/shard_map/ppermute | solution.py:27
  334.4 5.5 %collective-permute-start.8 = (f32[1,48,224]{2,1,0:T(8,128)S(1)}, f32[1,48,224]{2,1,0:T(8,128)S(1)}, u32[]{:S(2)}, u32[]{:S(2)}) collective-permute-start(f32[1,48,224]{2,1,0:T(8,128)S(1)} %get-tuple-element.16), channel_id=1, source_target_pairs={{0,1},{1,2},{2,3},{3,4},{4,5},{5,6},{6,7},{8,9},{9,10},{10,11},{11... | collective-permute-start | bytes 129032 | tf_op jit(solution)/shard_map/ppermute | solution.py:25
  338.0 5.4 %collective-permute-start.9 = (f32[1,48,224]{2,1,0:T(8,128)S(1)}, f32[1,48,224]{2,1,0:T(8,128)S(1)}, u32[]{:S(2)}, u32[]{:S(2)}) collective-permute-start(f32[1,48,224]{2,1,0:T(8,128)S(1)} %get-tuple-element.17), channel_id=1, source_target_pairs={{1,0},{2,1},{3,2},{4,3},{5,4},{6,5},{7,6},{9,8},{10,9},{11,10},{12... | collective-permute-start | bytes 129032 | tf_op jit(solution)/shard_map/ppermute | solution.py:27
  343.5 5.5 %collective-permute-start.10 = (f32[34,1,224]{2,1,0:T(1,128)S(1)}, f32[34,1,224]{2,1,0:T(1,128)S(1)}, u32[]{:S(2)}, u32[]{:S(2)}) collective-permute-start(f32[34,1,224]{2,1,0:T(1,128)S(1)} %get-tuple-element.11), channel_id=1, source_target_pairs={{0,8},{8,16},{16,24},{24,32},{32,40},{40,48},{48,56},{56,64},{64,7... | collective-permute-start | bytes 91400 | tf_op jit(solution)/shard_map/ppermute | solution.py:25
  347.5 4.8 %collective-permute-start.11 = (f32[34,1,224]{2,1,0:T(1,128)S(1)}, f32[34,1,224]{2,1,0:T(1,128)S(1)}, u32[]{:S(2)}, u32[]{:S(2)}) collective-permute-start(f32[34,1,224]{2,1,0:T(1,128)S(1)} %get-tuple-element.10), channel_id=1, source_target_pairs={{8,0},{16,8},{24,16},{32,24},{40,32},{48,40},{56,48},{64,56},{72,6... | collective-permute-start | bytes 91400 | tf_op jit(solution)/shard_map/ppermute | solution.py:27
Sparse Core Ops, SparseCore 0:
  14.1 255.6 all-reduce.1
where the time goes:
time: 366 us; the launch traced here: 363 us
  waiting for transfers between devices  280 us (77%)
  starting transfers between devices  30.8 us (8%)
  other arithmetic  24.9 us (7%)
  between operations  14.4 us (4%)
  matrix products  10.9 us (3%)
    psum x1, waiting for transfers between devices, body(): total = lax.psum(local, ('wide', 'narrow'))  260 us
    ppermute x6, starting transfers between devices, with_halo(): lax.ppermute(tail, axis, [(i, (i + 1) % count) for i in range(ends)])  21 us
    ppermute x6, waiting for transfers between devices, with_halo(): lax.ppermute(head, axis, [((i + 1) % count, i) for i in range(ends)])  19.9 us
    ppermute x6, starting transfers between devices, with_halo(): lax.ppermute(head, axis, [((i + 1) % count, i) for i in range(ends)])  9.81 us
    another operation x12, other arithmetic, subspace(): lower = jnp.linalg.cholesky(inner)  8.57 us
    another operation x8, other arithmetic, subspace(): basis = jax.scipy.linalg.solve_triangular(lower, grown.T, lower=True).T  7.51 us
  transfers between devices with their start and end apart: 13, of which 7 were waited for; matrix products, arithmetic and copies ran while one was open for 0% of the time, Pallas kernels for 0%

commit v1 on v0

v1 whole, which is shorter than its diff:
```python
import functools

import jax
import jax.numpy as jnp
import numpy as np
from jax import lax
from jax.experimental import pallas as pl
from jax.experimental.pallas import tpu as pltpu
from jax.sharding import PartitionSpec as P

TILE_ROWS = 32
TILE_COLS = 48
PIXELS = TILE_ROWS * TILE_COLS
BANDS = 224
RANK = 16
POWER_ITERS = 4
TV_ITERS = 3
CHIPS_X = 4
CHIPS_Z = 8
N_NARROW = 8
N_WIDE = CHIPS_X * CHIPS_Z
PLANE = CHIPS_X * N_NARROW
TOTAL_PIXELS = PIXELS * N_NARROW * N_WIDE
DEPTH = TV_ITERS
BORDER = DEPTH * TILE_COLS
SIDE = TILE_ROWS * 4
TOP, BOTTOM, LEFT, RIGHT, CORNER = 0, BORDER, 2 * BORDER, 2 * BORDER + SIDE, 2 * BORDER + 2 * SIDE
HALO = CORNER + 64
EXT_ROWS = TILE_ROWS + 2 * DEPTH
EXT_COLS = TILE_COLS + 16

MESH = pl.DeviceIdType.MESH
HIGHEST = lax.Precision.HIGHEST
F32 = jnp.float32
BF16 = jnp.bfloat16
TN = (((0,), (0,)), ((), ()))
NT = (((1,), (1,)), ((), ()))


def select_columns(pixels, first):
    shape = (SIDE, TILE_ROWS * 16)
    want = lax.broadcasted_iota(jnp.int32, shape, 0)
    have = lax.broadcasted_iota(jnp.int32, shape, 1)
    pick = (have == (want // 4) * 16 + want % 4 + first).astype(F32).astype(BF16)
    flat = pixels.reshape(TILE_ROWS * 16, BANDS)
    return jnp.dot(pick, flat, preferred_element_type=F32).astype(BF16)


def exchange_kernel(
    cube_ref, gram_ref, halo_ref,
    tile, packed, around, own, along, summed, edge_l, edge_r, halo,
    load_sem, send_sem, recv_sem, halo_send, halo_recv,
):
    wide = lax.axis_index("wide")
    narrow = lax.axis_index("narrow")
    z = wide // CHIPS_X
    x = wide % CHIPS_X
    block = x * N_NARROW + narrow

    load = pltpu.make_async_copy(cube_ref, tile, load_sem)
    load.start()

    def in_plane(step):
        other = (block + step) % PLANE
        return (z * CHIPS_X + other // N_NARROW, other % N_NARROW), other

    def on_line(step):
        return (((z + step) % CHIPS_Z) * CHIPS_X + x, narrow)

    def beside(dr, dc):
        return ((wide + dc + N_WIDE) % N_WIDE, (narrow + dr + N_NARROW) % N_NARROW)

    barrier = pltpu.get_barrier_semaphore()

    @pl.loop(1, PLANE)
    def _(step):
        pl.semaphore_signal(barrier, inc=1, device_id=in_plane(step)[0], device_id_type=MESH)

    @pl.loop(1, CHIPS_Z)
    def _(step):
        pl.semaphore_signal(barrier, inc=1, device_id=on_line(step), device_id_type=MESH)

    for dr in (-1, 0, 1):
        for dc in (-1, 0, 1):
            if dr or dc:
                pl.semaphore_signal(barrier, inc=1, device_id=beside(dr, dc), device_id_type=MESH)

    load.wait()
    values = tile[...]
    local = lax.dot_general(values, values, TN, preferred_element_type=F32)
    row = lax.broadcasted_iota(jnp.int32, (128, 128), 0)
    col = lax.broadcasted_iota(jnp.int32, (128, 128), 1)
    first = local[:128, :128]
    cross = jnp.concatenate([local[:128, 128:], jnp.zeros((128, 32), F32)], axis=1)
    last = jnp.concatenate([local[128:, 128:], jnp.zeros((96, 32), F32)], axis=1)
    last = jnp.concatenate([last, jnp.zeros((32, 128), F32)], axis=0)
    diagonal = jnp.sum(jnp.where(row == col, last, 0.0), axis=1, keepdims=True)
    packed[:16] = jnp.where(row <= col, first, last).reshape(16, 8, 128)
    packed[16:] = jnp.where(col == 96, diagonal, cross).reshape(16, 8, 128)

    pl.semaphore_wait(barrier, PLANE - 1 + CHIPS_Z - 1 + 8)

    @pl.loop(1, PLANE)
    def _(step):
        device, other = in_plane(step)
        pltpu.make_async_remote_copy(
            src_ref=packed.at[other], dst_ref=around.at[step - 1],
            send_sem=send_sem.at[0], recv_sem=recv_sem.at[0],
            device_id=device, device_id_type=MESH,
        ).start()

    grid = values.reshape(TILE_ROWS, TILE_COLS, BANDS)
    edge_l[...] = select_columns(grid[:, :16], 0)
    edge_r[...] = select_columns(grid[:, 32:], 12)
    pieces = (
        (-1, 0, tile.at[pl.ds(0, BORDER)], BOTTOM, BORDER),
        (1, 0, tile.at[pl.ds(PIXELS - BORDER, BORDER)], TOP, BORDER),
        (0, -1, edge_l, RIGHT, SIDE),
        (0, 1, edge_r, LEFT, SIDE),
        (-1, -1, edge_l.at[pl.ds(0, 16)], CORNER + 48, 16),
        (1, -1, edge_l.at[pl.ds(SIDE - 16, 16)], CORNER + 16, 16),
        (-1, 1, edge_r.at[pl.ds(0, 16)], CORNER + 32, 16),
        (1, 1, edge_r.at[pl.ds(SIDE - 16, 16)], CORNER, 16),
    )
    borders = []
    for index, (dr, dc, source, at, size) in enumerate(pieces):
        copy = pltpu.make_async_remote_copy(
            src_ref=source, dst_ref=halo.at[pl.ds(at, size)],
            send_sem=halo_send.at[index], recv_sem=halo_recv.at[index],
            device_id=beside(dr, dc), device_id_type=MESH,
        )
        copy.start()
        borders.append(copy)

    def wait_for(ref, count, sem):
        part = ref.at[pl.ds(0, count)]
        pltpu.make_async_copy(part, part, sem).wait()

    wait_for(around, PLANE - 1, recv_sem.at[0])
    total = packed[block]
    for step in range(PLANE - 1):
        total = total + around[step]
    own[...] = total
    along[z] = total

    @pl.loop(1, CHIPS_Z)
    def _(step):
        pltpu.make_async_remote_copy(
            src_ref=own, dst_ref=along.at[z],
            send_sem=send_sem.at[1], recv_sem=recv_sem.at[1],
            device_id=on_line(step), device_id_type=MESH,
        ).start()

    wait_for(along, CHIPS_Z - 1, recv_sem.at[1])
    total = along[0]
    for step in range(1, CHIPS_Z):
        total = total + along[step]
    summed[block] = total

    @pl.loop(1, PLANE)
    def _(step):
        device, other = in_plane(step)
        pltpu.make_async_remote_copy(
            src_ref=summed.at[block], dst_ref=summed.at[block],
            send_sem=send_sem.at[2], recv_sem=recv_sem.at[2],
            device_id=device, device_id_type=MESH,
        ).start()

    for copy in borders:
        copy.wait_recv()
    halo_ref[...] = halo[...]
    wait_for(summed, PLANE - 1, recv_sem.at[2])
    gram_ref[...] = summed[...].reshape(256, 128)
    wait_for(packed, PLANE - 1, send_sem.at[0])
    wait_for(along, CHIPS_Z - 1, send_sem.at[1])
    wait_for(summed, PLANE - 1, send_sem.at[2])
    for copy in borders:
        copy.wait_send()


def exchange(cube):
    return pl.pallas_call(
        exchange_kernel,
        out_shape=(
            jax.ShapeDtypeStruct((256, 128), F32),
            jax.ShapeDtypeStruct((HALO, BANDS), BF16),
        ),
        in_specs=[pl.BlockSpec(memory_space=pl.ANY)],
        out_specs=(pl.BlockSpec(memory_space=pltpu.VMEM), pl.BlockSpec(memory_space=pltpu.VMEM)),
        scratch_shapes=[
            pltpu.VMEM((PIXELS, BANDS), BF16),
            pltpu.VMEM((PLANE, 8, 128), F32),
            pltpu.VMEM((PLANE, 8, 128), F32),
            pltpu.VMEM((8, 128), F32),
            pltpu.VMEM((CHIPS_Z, 8, 128), F32),
            pltpu.VMEM((PLANE, 8, 128), F32),
            pltpu.VMEM((SIDE, BANDS), BF16),
            pltpu.VMEM((SIDE, BANDS), BF16),
            pltpu.VMEM((HALO, BANDS), BF16),
            pltpu.SemaphoreType.DMA,
            pltpu.SemaphoreType.DMA((3,)),
            pltpu.SemaphoreType.DMA((3,)),
            pltpu.SemaphoreType.DMA((8,)),
            pltpu.SemaphoreType.DMA((8,)),
        ],
        compiler_params=pltpu.CompilerParams(collective_id=0, has_side_effects=True),
    )(cube)


def split(values):
    high = values.astype(BF16)
    return high, (values - high.astype(F32)).astype(BF16)


def subspace(packed, start):
    row = lax.broadcasted_iota(jnp.int32, (128, 128), 0)
    col = lax.broadcasted_iota(jnp.int32, (128, 128), 1)
    packed = packed * (1.0 / TOTAL_PIXELS)
    mixed, cross = packed[:128], packed[128:]
    flipped = mixed.T
    first = jnp.where(row <= col, mixed, flipped)
    inside = (row < 96) & (col < 96)
    last = jnp.where(inside, jnp.where(row > col, mixed, flipped), 0.0)
    last = jnp.where(inside & (row == col), cross[:, 96:97], last)
    cross = jnp.where(col < 96, cross, 0.0)
    gram = jnp.concatenate(
        [jnp.concatenate([first, cross], axis=1), jnp.concatenate([cross.T, last], axis=1)], axis=0
    )
    rank_row = lax.broadcasted_iota(jnp.int32, (RANK, 1), 0)
    basis = start
    for _ in range(POWER_ITERS):
        grown = jnp.dot(basis, gram, precision=HIGHEST, preferred_element_type=F32)
        inner = lax.dot_general(grown, grown, NT, precision=HIGHEST, preferred_element_type=F32)
        scale = jnp.zeros((RANK, 1), F32)
        for step in range(RANK):
            pivot = inner[step : step + 1, step : step + 1]
            scale = jnp.where(rank_row == step, lax.rsqrt(pivot), scale)
            if step < RANK - 1:
                factor = jnp.where(rank_row > step, inner[:, step : step + 1] / pivot, 0.0)
                inner = inner - factor * inner[step : step + 1, :]
                grown = grown - factor * grown[step : step + 1, :]
        basis = grown * scale
    return basis


def smooth_kernel(gram_ref, halo_ref, cube_ref, start_ref, out_ref, proj_ref, u0, u1, u2, flow):
    wide = lax.axis_index("wide")
    narrow = lax.axis_index("narrow")
    basis = subspace(gram_ref[...], start_ref[...])
    proj_ref[...] = lax.dot_general(
        basis, basis, TN, precision=HIGHEST, preferred_element_type=F32
    )[:BANDS, :BANDS]
    low = basis.astype(BF16).astype(F32)
    fit = 4.0 * lax.dot_general(low, basis, TN, precision=HIGHEST, preferred_element_type=F32)
    high, rest = split(fit[:BANDS])

    def fitted(pixels):
        return jnp.dot(pixels, high, preferred_element_type=F32) + jnp.dot(
            pixels, rest, preferred_element_type=F32
        )

    def put(values, rows, row, col, count):
        for half in range(2):
            part = values[:, half * 128 : (half + 1) * 128]
            for r in range(rows):
                u0[half, row + r, col : col + count, :] = part[r * count : (r + 1) * count]

    put(fitted(halo_ref[TOP : TOP + BORDER]), DEPTH, 0, 8, TILE_COLS)
    put(fitted(halo_ref[BOTTOM : BOTTOM + BORDER]), DEPTH, DEPTH + TILE_ROWS, 8, TILE_COLS)
    put(fitted(halo_ref[LEFT : LEFT + SIDE]), TILE_ROWS, DEPTH, 4, 4)
    put(fitted(halo_ref[RIGHT : RIGHT + SIDE]), TILE_ROWS, DEPTH, 8 + TILE_COLS, 4)
    corners = fitted(halo_ref[CORNER : CORNER + 64])
    put(corners[4:16], DEPTH, 0, 4, 4)
    put(corners[20:32], DEPTH, 0, 8 + TILE_COLS, 4)
    put(corners[32:44], DEPTH, DEPTH + TILE_ROWS, 4, 4)
    put(corners[48:60], DEPTH, DEPTH + TILE_ROWS, 8 + TILE_COLS, 4)

    @pl.loop(0, TILE_ROWS // 4)
    def _(index):
        at = pl.multiple_of(index * (4 * TILE_COLS), 4 * TILE_COLS)
        values = fitted(cube_ref[pl.ds(at, 4 * TILE_COLS), :])
        put(values, 4, DEPTH + index * 4, 8, TILE_COLS)

    stages = (u0, u1, u2)
    for turn in range(TV_ITERS):
        here = stages[turn]

        @pl.when(narrow == 0)
        def _():
            here[:, DEPTH - 1] = here[:, DEPTH]

        @pl.when(narrow == N_NARROW - 1)
        def _():
            here[:, DEPTH + TILE_ROWS] = here[:, DEPTH + TILE_ROWS - 1]

        @pl.when(wide == 0)
        def _():
            here[:, :, 7:8, :] = here[:, :, 8:9, :]

        @pl.when(wide == N_WIDE - 1)
        def _():
            here[:, :, 8 + TILE_COLS : 9 + TILE_COLS, :] = here[:, :, 7 + TILE_COLS : 8 + TILE_COLS, :]

        last = turn == TV_ITERS - 1
        for half in range(2):

            def flows(row):
                middle = here[half, row, 0:EXT_COLS, :]
                gx = here[half, row + 1, 0:EXT_COLS, :] - middle
                gy = here[half, row, 1 : EXT_COLS + 1, :] - middle
                scale = lax.rsqrt(gx * gx + gy * gy + 4.0)
                return middle, gx * scale, gy * scale

            def line(row, above):
                middle, px, py = flows(row)
                flow[8 : 8 + EXT_COLS, :] = py
                change = px - above + (py - flow[7 : 7 + EXT_COLS, :])
                if turn == 0:
                    value = middle + change
                else:
                    value = 0.5 * (middle + u0[half, row, 0:EXT_COLS, :]) + change
                if last:
                    width = 128 if half == 0 else BANDS - 128
                    at = pl.multiple_of((row - DEPTH) * TILE_COLS, TILE_COLS)
                    out_ref[pl.ds(at, TILE_COLS), half * 128 : half * 128 + width] = (
                        0.25 * value[8 : 8 + TILE_COLS, :width]
                    ).astype(BF16)
                else:
                    stages[turn + 1][half, row, 0:EXT_COLS, :] = value
                return px

            lax.fori_loop(turn + 1, EXT_ROWS - 1 - turn, line, flows(turn)[1])


def smooth(gram, halo, cube, start):
    vmem = pl.BlockSpec(memory_space=pltpu.VMEM)
    field = pltpu.VMEM((2, EXT_ROWS, EXT_COLS + 8, 128), F32)
    return pl.pallas_call(
        smooth_kernel,
        out_shape=(
            jax.ShapeDtypeStruct((PIXELS, BANDS), BF16),
            jax.ShapeDtypeStruct((BANDS, BANDS), F32),
        ),
        in_specs=[vmem] * 4,
        out_specs=(vmem, vmem),
        scratch_shapes=[field, field, field, pltpu.VMEM((EXT_COLS + 16, 128), F32)],
    )(gram, halo, cube, start)


def first_basis():
    bands = np.arange(256)[None, :]
    cols = np.arange(RANK)[:, None]
    values = np.cos(np.pi * (bands + 0.5) * cols / BANDS)
    return np.where(bands < BANDS, values, 0.0).astype(np.float32)


def body(cube):
    flat = cube.reshape(PIXELS, BANDS)
    gram, halo = exchange(flat)
    restored, projector = smooth(gram, halo, flat, jnp.asarray(first_basis()))
    return restored.reshape(TILE_ROWS, TILE_COLS, BANDS), projector


def solution(mesh):
    return jax.shard_map(
        body,
        mesh=mesh,
        in_specs=(P("narrow", "wide", None),),
        out_specs=(P("narrow", "wide", None), P()),
        check_vma=False,
    )
```

time: 366 us -> 47.5 us (0.13)
  waiting for transfers between devices: 280 us -> 0 us
  Pallas kernels: 0 us -> 46.7 us
  starting transfers between devices: 30.8 us -> 0 us
  other arithmetic: 24.9 us -> 0 us
  between operations: 14.4 us -> 0.64 us
  matrix products: 10.9 us -> 0 us
    psum x1 -> x0, waiting for transfers between devices: 260 us -> none  [body(): total = lax.psum(local, ('wide', 'narrow'))]
    pallas_call x0 -> x2, Pallas kernels: none -> 46.7 us  [the longest x1 28.4 us: exchange(): pl.pallas_call(exchange_kernel, out_shape=(jax.ShapeDtypeStruct((256, 128...]
    ppermute x12 -> x0, starting transfers between devices: 30.8 us -> none  [the longest x6 21 us: with_halo(): lax.ppermute(tail, axis, [(i, (i + 1) % count) for i in range(ends)])]
    ppermute x12 -> x0, waiting for transfers between devices: 19.9 us -> none  [the longest x6 19.9 us: with_halo(): lax.ppermute(head, axis, [((i + 1) % count, i) for i in range(ends)])]
    another operation x20 -> x0, other arithmetic: 16.1 us -> none  [the longest x12 8.57 us: subspace(): lower = jnp.linalg.cholesky(inner)]
    dot_general x12 -> x0, matrix products: 10.1 us -> none  [the longest x4 5.3 us: subspace(): grown = jnp.dot(gram, basis, precision=hi_prec)]
    div x7 -> x0, other arithmetic: 4.23 us -> none  [the longest x3 4.2 us: smooth_step(): flow_x = grad_x / magnitude]
  transfers between devices with their start and end apart: 13 -> 0, of which waited for: 7 -> 0; matrix products, arithmetic and copies ran while one was open for 0% -> 0% of each run, Pallas kernels for 0% -> 0%
where the time goes in v1:
time: 47.5 us; the launch traced here: 47.4 us
  Pallas kernels  46.7 us (98%)
  between operations  0.64 us (1%)
    pallas_call x1, Pallas kernels, exchange(): pl.pallas_call(exchange_kernel, out_shape=(jax.ShapeDtypeStruct((256, 128...  28.4 us
    pallas_call x1, Pallas kernels, smooth(): pl.pallas_call(smooth_kernel, out_shape=(jax.ShapeDtypeStruct((PIXELS, BA...  18.3 us

profile of v1, /device:TPU:1, one launch (start us, length us, event | category | flops | bytes accessed | tf_op | source)
XLA Modules:
  0.0 47.4 jit_solution(8642005114760194353)
XLA Ops:
  0.6 28.4 %shard_map.41 = (f32[256,128]{1,0:T(8,128)}, bf16[608,224]{1,0:T(8,128)(2,1)}) custom-call(bf16[1536,224]{1,0:T(8,128)(2,1)} %bitcast.2), custom_call_target="tpu_custom_call" | custom-call | tf_op jit(solution)/shard_map/pallas_call | solution.py:182
  29.0 18.3 %shard_map.42 = (bf16[1536,224]{1,0:T(8,128)(2,1)}, f32[224,224]{1,0:T(8,128)}) custom-call(f32[256,128]{1,0:T(8,128)} %get-tuple-element.6.gram_ref, bf16[608,224]{1,0:T(8,128)(2,1)} %get-tuple-element.7.halo_ref, bf16[1536,224]{1,0:T(8,128)(2,1)} %bitcast.3, f32[16,256]{1,0:T(8,128)} %constant.2.clone.start_ref), custom_call_target="tpu_custom_call" | custom-call | tf_op jit(solution)/shard_map/pallas_call | solution.py:338

commit v2 on v1

--- a/solution.py
+++ b/solution.py
@@ -209,10 +209,12 @@
 
 def split(values):
     high = values.astype(BF16)
-    return high, (values - high.astype(F32)).astype(BF16)
-
-
-def subspace(packed, start):
+    values = values - high.astype(F32)
+    middle = values.astype(BF16)
+    return high, middle, (values - middle.astype(F32)).astype(BF16)
+
+
+def unpack(packed):
     row = lax.broadcasted_iota(jnp.int32, (128, 128), 0)
     col = lax.broadcasted_iota(jnp.int32, (128, 128), 1)
     packed = packed * (1.0 / TOTAL_PIXELS)
@@ -223,36 +225,67 @@
     last = jnp.where(inside, jnp.where(row > col, mixed, flipped), 0.0)
     last = jnp.where(inside & (row == col), cross[:, 96:97], last)
     cross = jnp.where(col < 96, cross, 0.0)
-    gram = jnp.concatenate(
+    return jnp.concatenate(
         [jnp.concatenate([first, cross], axis=1), jnp.concatenate([cross.T, last], axis=1)], axis=0
     )
-    rank_row = lax.broadcasted_iota(jnp.int32, (RANK, 1), 0)
+
+
+def orthonormal(inner, grown):
+    row = lax.broadcasted_iota(jnp.int32, (RANK, 128), 0)
+    cols = [jnp.broadcast_to(inner[:, k : k + 1], (RANK, 128)) for k in range(RANK)]
+    halves = [grown[:, :128], grown[:, 128:]]
+    pivots = jnp.zeros((RANK, 128), F32)
+    for step in range(RANK):
+        pivot = cols[step][step : step + 1]
+        pivots = jnp.where(row == step, pivot, pivots)
+        if step < RANK - 1:
+            factor = jnp.where(row > step, cols[step] * (1.0 / pivot), 0.0)
+            for k in range(step + 1, RANK):
+                cols[k] = cols[k] - factor * cols[k][step : step + 1]
+            halves = [half - factor * half[step : step + 1] for half in halves]
+    scale = lax.rsqrt(pivots)
+    return jnp.concatenate([half * scale for half in halves], axis=1)
+
+
+def subspace(packed, start):
+    gram = split(unpack(packed))
     basis = start
     for _ in range(POWER_ITERS):
-        grown = jnp.dot(basis, gram, precision=HIGHEST, preferred_element_type=F32)
-        inner = lax.dot_general(grown, grown, NT, precision=HIGHEST, preferred_element_type=F32)
-        scale = jnp.zeros((RANK, 1), F32)
-        for step in range(RANK):
-            pivot = inner[step : step + 1, step : step + 1]
-            scale = jnp.where(rank_row == step, lax.rsqrt(pivot), scale)
-            if step < RANK - 1:
-                factor = jnp.where(rank_row > step, inner[:, step : step + 1] / pivot, 0.0)
-                inner = inner - factor * inner[step : step + 1, :]
-                grown = grown - factor * grown[step : step + 1, :]
-        basis = grown * scale
+        high, middle, low = split(basis)
+        parts = jnp.dot(jnp.concatenate([high, middle, low], axis=0), gram[0], preferred_element_type=F32)
+        more = jnp.dot(jnp.concatenate([high, middle], axis=0), gram[1], preferred_element_type=F32)
+        least = jnp.dot(high, gram[2], preferred_element_type=F32)
+        grown = (
+            (parts[2 * RANK :] + more[RANK:] + least)
+            + (parts[RANK : 2 * RANK] + more[:RANK])
+            + parts[:RANK]
+        )
+        high, middle, low = split(grown)
+        inner = lax.dot_general(
+            jnp.concatenate([low, high, middle, middle, high, high], axis=1),
+            jnp.concatenate([high, low, middle, high, middle, high], axis=1),
+            NT, preferred_element_type=F32,
+        )
+        basis = orthonormal(inner, grown)
     return basis
 
 
-def smooth_kernel(gram_ref, halo_ref, cube_ref, start_ref, out_ref, proj_ref, u0, u1, u2, flow):
+def smooth_kernel(
+    gram_ref, halo_hbm, cube_hbm, start_ref, out_ref, proj_ref, u0, u1, u2, flow, halo_ref, cube_ref, sems
+):
     wide = lax.axis_index("wide")
     narrow = lax.axis_index("narrow")
+    load_cube = pltpu.make_async_copy(cube_hbm, cube_ref, sems.at[0])
+    load_halo = pltpu.make_async_copy(halo_hbm, halo_ref, sems.at[1])
+    load_cube.start()
+    load_halo.start()
     basis = subspace(gram_ref[...], start_ref[...])
+    low = basis.astype(BF16).astype(F32)
+    fit = 4.0 * lax.dot_general(low, basis, TN, precision=HIGHEST, preferred_element_type=F32)
+    high, rest, _ = split(fit[:BANDS])
     proj_ref[...] = lax.dot_general(
         basis, basis, TN, precision=HIGHEST, preferred_element_type=F32
     )[:BANDS, :BANDS]
-    low = basis.astype(BF16).astype(F32)
-    fit = 4.0 * lax.dot_general(low, basis, TN, precision=HIGHEST, preferred_element_type=F32)
-    high, rest = split(fit[:BANDS])
 
     def fitted(pixels):
         return jnp.dot(pixels, high, preferred_element_type=F32) + jnp.dot(
@@ -265,25 +298,29 @@
             for r in range(rows):
                 u0[half, row + r, col : col + count, :] = part[r * count : (r + 1) * count]
 
-    put(fitted(halo_ref[TOP : TOP + BORDER]), DEPTH, 0, 8, TILE_COLS)
-    put(fitted(halo_ref[BOTTOM : BOTTOM + BORDER]), DEPTH, DEPTH + TILE_ROWS, 8, TILE_COLS)
-    put(fitted(halo_ref[LEFT : LEFT + SIDE]), TILE_ROWS, DEPTH, 4, 4)
-    put(fitted(halo_ref[RIGHT : RIGHT + SIDE]), TILE_ROWS, DEPTH, 8 + TILE_COLS, 4)
-    corners = fitted(halo_ref[CORNER : CORNER + 64])
+    load_cube.wait()
+    load_halo.wait()
+
+    @pl.loop(0, TILE_ROWS // 8)
+    def _(index):
+        at = pl.multiple_of(index * (8 * TILE_COLS), 8 * TILE_COLS)
+        put(fitted(cube_ref[pl.ds(at, 8 * TILE_COLS), :]), 8, DEPTH + index * 8, 8, TILE_COLS)
+
+    borders = fitted(halo_ref[...])
+    put(borders[TOP : TOP + BORDER], DEPTH, 0, 8, TILE_COLS)
+    put(borders[BOTTOM : BOTTOM + BORDER], DEPTH, DEPTH + TILE_ROWS, 8, TILE_COLS)
+    put(borders[LEFT : LEFT + SIDE], TILE_ROWS, DEPTH, 4, 4)
+    put(borders[RIGHT : RIGHT + SIDE], TILE_ROWS, DEPTH, 8 + TILE_COLS, 4)
+    corners = borders[CORNER:]
     put(corners[4:16], DEPTH, 0, 4, 4)
     put(corners[20:32], DEPTH, 0, 8 + TILE_COLS, 4)
     put(corners[32:44], DEPTH, DEPTH + TILE_ROWS, 4, 4)
     put(corners[48:60], DEPTH, DEPTH + TILE_ROWS, 8 + TILE_COLS, 4)
 
-    @pl.loop(0, TILE_ROWS // 4)
-    def _(index):
-        at = pl.multiple_of(index * (4 * TILE_COLS), 4 * TILE_COLS)
-        values = fitted(cube_ref[pl.ds(at, 4 * TILE_COLS), :])
-        put(values, 4, DEPTH + index * 4, 8, TILE_COLS)
-
     stages = (u0, u1, u2)
     for turn in range(TV_ITERS):
         here = stages[turn]
+        final = turn == TV_ITERS - 1
 
         @pl.when(narrow == 0)
         def _():
@@ -301,39 +338,47 @@
         def _():
             here[:, :, 8 + TILE_COLS : 9 + TILE_COLS, :] = here[:, :, 7 + TILE_COLS : 8 + TILE_COLS, :]
 
-        last = turn == TV_ITERS - 1
-        for half in range(2):
-
-            def flows(row):
-                middle = here[half, row, 0:EXT_COLS, :]
-                gx = here[half, row + 1, 0:EXT_COLS, :] - middle
-                gy = here[half, row, 1 : EXT_COLS + 1, :] - middle
-                scale = lax.rsqrt(gx * gx + gy * gy + 4.0)
-                return middle, gx * scale, gy * scale
-
-            def line(row, above):
-                middle, px, py = flows(row)
-                flow[8 : 8 + EXT_COLS, :] = py
-                change = px - above + (py - flow[7 : 7 + EXT_COLS, :])
-                if turn == 0:
-                    value = middle + change
-                else:
-                    value = 0.5 * (middle + u0[half, row, 0:EXT_COLS, :]) + change
-                if last:
-                    width = 128 if half == 0 else BANDS - 128
-                    at = pl.multiple_of((row - DEPTH) * TILE_COLS, TILE_COLS)
-                    out_ref[pl.ds(at, TILE_COLS), half * 128 : half * 128 + width] = (
-                        0.25 * value[8 : 8 + TILE_COLS, :width]
-                    ).astype(BF16)
-                else:
-                    stages[turn + 1][half, row, 0:EXT_COLS, :] = value
-                return px
-
-            lax.fori_loop(turn + 1, EXT_ROWS - 1 - turn, line, flows(turn)[1])
+        first, count = (8, TILE_COLS) if final else (4, TILE_COLS + 8)
+
+        def flows(half, row, at, size):
+            middle = here[half, row, at : at + size, :]
+            gx = here[half, row + 1, at : at + size, :] - middle
+            gy = here[half, row, at + 1 : at + 1 + size, :] - middle
+            scale = lax.rsqrt(gx * gx + gy * gy + 4.0)
+            return middle, gx * scale, gy * scale
+
+        def pair(index, above):
+            above = list(above)
+            for lane in range(2):
+                row = turn + 1 + 2 * index + lane
+                for half in range(2):
+                    middle, px, py = flows(half, row, first, count)
+                    flow[lane, half, 8 : 8 + count, :] = py
+                    if final:
+                        flow[lane, half, 0:8, :] = flows(half, row, 0, 8)[2]
+                    change = px - above[half] + (py - flow[lane, half, 7 : 7 + count, :])
+                    above[half] = px
+                    if turn == 0:
+                        value = middle + change
+                    else:
+                        value = 0.5 * (middle + u0[half, row, first : first + count, :]) + change
+                    if final:
+                        width = 128 if half == 0 else BANDS - 128
+                        at = pl.multiple_of((row - DEPTH) * TILE_COLS, TILE_COLS)
+                        out_ref[pl.ds(at, TILE_COLS), half * 128 : half * 128 + width] = (
+                            0.25 * value[:, :width]
+                        ).astype(BF16)
+                    else:
+                        stages[turn + 1][half, row, first : first + count, :] = value
+            return tuple(above)
+
+        start = tuple(flows(half, turn, first, count)[1] for half in range(2))
+        lax.fori_loop(0, (EXT_ROWS - 2 - 2 * turn) // 2, pair, start)
 
 
 def smooth(gram, halo, cube, start):
     vmem = pl.BlockSpec(memory_space=pltpu.VMEM)
+    hbm = pl.BlockSpec(memory_space=pl.ANY)
     field = pltpu.VMEM((2, EXT_ROWS, EXT_COLS + 8, 128), F32)
     return pl.pallas_call(
         smooth_kernel,
@@ -341,9 +386,15 @@
             jax.ShapeDtypeStruct((PIXELS, BANDS), BF16),
             jax.ShapeDtypeStruct((BANDS, BANDS), F32),
         ),
-        in_specs=[vmem] * 4,
+        in_specs=[vmem, hbm, hbm, vmem],
         out_specs=(vmem, vmem),
-        scratch_shapes=[field, field, field, pltpu.VMEM((EXT_COLS + 16, 128), F32)],
+        scratch_shapes=[
+            field, field, field,
+            pltpu.VMEM((2, 2, EXT_COLS + 16, 128), F32),
+            pltpu.VMEM((HALO, BANDS), BF16),
+            pltpu.VMEM((PIXELS, BANDS), BF16),
+            pltpu.SemaphoreType.DMA((2,)),
+        ],
     )(gram, halo, cube, start)
 
 

time: 47.5 us -> 40 us (0.84)
  Pallas kernels: 46.7 us -> 39.2 us
    pallas_call x1, Pallas kernels: 18.3 us -> 10.8 us  [smooth(): pl.pallas_call(smooth_kernel, out_shape=(jax.ShapeDtypeStruct((PIXELS, BA...]
where the time goes in v2:
time: 40 us; the launch traced here: 39.8 us
  Pallas kernels  39.2 us (98%)
  between operations  0.64 us (2%)
    pallas_call x1, Pallas kernels, exchange(): pl.pallas_call(exchange_kernel, out_shape=(jax.ShapeDtypeStruct((256, 128...  28.4 us
    pallas_call x1, Pallas kernels, smooth(): pl.pallas_call(smooth_kernel, out_shape=(jax.ShapeDtypeStruct((PIXELS, BA...  10.8 us

profile of v2, /device:TPU:1, one launch (start us, length us, event | category | flops | bytes accessed | tf_op | source)
XLA Modules:
  0.0 39.8 jit_solution(14869932859289189015)
XLA Ops:
  0.6 28.4 %shard_map.41 = (f32[256,128]{1,0:T(8,128)}, bf16[608,224]{1,0:T(8,128)(2,1)}) custom-call(bf16[1536,224]{1,0:T(8,128)(2,1)} %bitcast.2), custom_call_target="tpu_custom_call" | custom-call | tf_op jit(solution)/shard_map/pallas_call | solution.py:182
  29.0 10.8 %shard_map.42 = (bf16[1536,224]{1,0:T(8,128)(2,1)}, f32[224,224]{1,0:T(8,128)}) custom-call(f32[256,128]{1,0:T(8,128)} %get-tuple-element.6.gram_ref, bf16[608,224]{1,0:T(8,128)(2,1)} %get-tuple-element.7.halo_hbm, bf16[1536,224]{1,0:T(8,128)(2,1)} %bitcast.3, f32[16,256]{1,0:T(8,128)} %constant.2.clone.start_ref), custom_call_target="tpu_custom_call" | custom-call | tf_op jit(solution)/shard_map/pallas_call | solution.py:383

commit v3 on v2

--- a/solution.py
+++ b/solution.py
@@ -29,6 +29,12 @@
 EXT_ROWS = TILE_ROWS + 2 * DEPTH
 EXT_COLS = TILE_COLS + 16
 
+PLANE_STEPS = sorted(
+    ((dx, dn) for dx in range(CHIPS_X) for dn in range(N_NARROW) if dx or dn),
+    key=lambda s: -(2 * min(s[0], CHIPS_X - s[0]) + min(s[1], N_NARROW - s[1])),
+)
+LINE_STEPS = sorted(range(1, CHIPS_Z), key=lambda s: -min(s, CHIPS_Z - s))
+
 MESH = pl.DeviceIdType.MESH
 HIGHEST = lax.Precision.HIGHEST
 F32 = jnp.float32
@@ -47,9 +53,9 @@
 
 
 def exchange_kernel(
-    cube_ref, gram_ref, halo_ref,
-    tile, packed, around, own, along, summed, edge_l, edge_r, halo,
-    load_sem, send_sem, recv_sem, halo_send, halo_recv,
+    cube_ref, first_ref, gram_ref, halo_ref, tile, start_ref,
+    packed, around, own, along, summed, edge_l, edge_r, halo,
+    load_sems, send_sem, recv_sem, halo_send, halo_recv,
 ):
     wide = lax.axis_index("wide")
     narrow = lax.axis_index("narrow")
@@ -57,12 +63,14 @@
     x = wide % CHIPS_X
     block = x * N_NARROW + narrow
 
-    load = pltpu.make_async_copy(cube_ref, tile, load_sem)
+    load = pltpu.make_async_copy(cube_ref, tile, load_sems.at[0])
     load.start()
-
-    def in_plane(step):
-        other = (block + step) % PLANE
-        return (z * CHIPS_X + other // N_NARROW, other % N_NARROW), other
+    load_first = pltpu.make_async_copy(first_ref, start_ref, load_sems.at[1])
+    load_first.start()
+
+    def in_plane(dx, dn):
+        other_x, other_n = (x + dx) % CHIPS_X, (narrow + dn) % N_NARROW
+        return (z * CHIPS_X + other_x, other_n), other_x * N_NARROW + other_n
 
     def on_line(step):
         return (((z + step) % CHIPS_Z) * CHIPS_X + x, narrow)
@@ -72,20 +80,17 @@
 
     barrier = pltpu.get_barrier_semaphore()
 
-    @pl.loop(1, PLANE)
-    def _(step):
-        pl.semaphore_signal(barrier, inc=1, device_id=in_plane(step)[0], device_id_type=MESH)
-
-    @pl.loop(1, CHIPS_Z)
-    def _(step):
+    for dx, dn in PLANE_STEPS:
+        pl.semaphore_signal(barrier, inc=1, device_id=in_plane(dx, dn)[0], device_id_type=MESH)
+    for step in LINE_STEPS:
         pl.semaphore_signal(barrier, inc=1, device_id=on_line(step), device_id_type=MESH)
-
     for dr in (-1, 0, 1):
         for dc in (-1, 0, 1):
             if dr or dc:
                 pl.semaphore_signal(barrier, inc=1, device_id=beside(dr, dc), device_id_type=MESH)
 
     load.wait()
+    load_first.wait()
     values = tile[...]
     local = lax.dot_general(values, values, TN, preferred_element_type=F32)
     row = lax.broadcasted_iota(jnp.int32, (128, 128), 0)
@@ -100,11 +105,10 @@
 
     pl.semaphore_wait(barrier, PLANE - 1 + CHIPS_Z - 1 + 8)
 
-    @pl.loop(1, PLANE)
-    def _(step):
-        device, other = in_plane(step)
+    for slot, (dx, dn) in enumerate(PLANE_STEPS):
+        device, other = in_plane(dx, dn)
         pltpu.make_async_remote_copy(
-            src_ref=packed.at[other], dst_ref=around.at[step - 1],
+            src_ref=packed.at[other], dst_ref=around.at[slot],
             send_sem=send_sem.at[0], recv_sem=recv_sem.at[0],
             device_id=device, device_id_type=MESH,
         ).start()
@@ -112,6 +116,25 @@
     grid = values.reshape(TILE_ROWS, TILE_COLS, BANDS)
     edge_l[...] = select_columns(grid[:, :16], 0)
     edge_r[...] = select_columns(grid[:, 32:], 12)
+
+    def wait_for(ref, count, sem):
+        part = ref.at[pl.ds(0, count)]
+        pltpu.make_async_copy(part, part, sem).wait()
+
+    wait_for(around, PLANE - 1, recv_sem.at[0])
+    total = packed[block]
+    for step in range(PLANE - 1):
+        total = total + around[step]
+    own[...] = total
+    along[z] = total
+
+    for step in LINE_STEPS:
+        pltpu.make_async_remote_copy(
+            src_ref=own, dst_ref=along.at[z],
+            send_sem=send_sem.at[1], recv_sem=recv_sem.at[1],
+            device_id=on_line(step), device_id_type=MESH,
+        ).start()
+
     pieces = (
         (-1, 0, tile.at[pl.ds(0, BORDER)], BOTTOM, BORDER),
         (1, 0, tile.at[pl.ds(PIXELS - BORDER, BORDER)], TOP, BORDER),
@@ -132,38 +155,17 @@
         copy.start()
         borders.append(copy)
 
-    def wait_for(ref, count, sem):
-        part = ref.at[pl.ds(0, count)]
-        pltpu.make_async_copy(part, part, sem).wait()
-
-    wait_for(around, PLANE - 1, recv_sem.at[0])
-    total = packed[block]
-    for step in range(PLANE - 1):
-        total = total + around[step]
-    own[...] = total
-    along[z] = total
-
-    @pl.loop(1, CHIPS_Z)
-    def _(step):
-        pltpu.make_async_remote_copy(
-            src_ref=own, dst_ref=along.at[z],
-            send_sem=send_sem.at[1], recv_sem=recv_sem.at[1],
-            device_id=on_line(step), device_id_type=MESH,
-        ).start()
-
     wait_for(along, CHIPS_Z - 1, recv_sem.at[1])
     total = along[0]
     for step in range(1, CHIPS_Z):
         total = total + along[step]
     summed[block] = total
 
-    @pl.loop(1, PLANE)
-    def _(step):
-        device, other = in_plane(step)
+    for dx, dn in PLANE_STEPS:
         pltpu.make_async_remote_copy(
             src_ref=summed.at[block], dst_ref=summed.at[block],
             send_sem=send_sem.at[2], recv_sem=recv_sem.at[2],
-            device_id=device, device_id_type=MESH,
+            device_id=in_plane(dx, dn)[0], device_id_type=MESH,
         ).start()
 
     for copy in borders:
@@ -178,17 +180,20 @@
         copy.wait_send()
 
 
-def exchange(cube):
+def exchange(cube, first):
+    vmem = pl.BlockSpec(memory_space=pltpu.VMEM)
+    hbm = pl.BlockSpec(memory_space=pltpu.HBM)
     return pl.pallas_call(
         exchange_kernel,
         out_shape=(
             jax.ShapeDtypeStruct((256, 128), F32),
             jax.ShapeDtypeStruct((HALO, BANDS), BF16),
+            jax.ShapeDtypeStruct((PIXELS, BANDS), BF16),
+            jax.ShapeDtypeStruct((RANK, 256), F32),
         ),
-        in_specs=[pl.BlockSpec(memory_space=pl.ANY)],
-        out_specs=(pl.BlockSpec(memory_space=pltpu.VMEM), pl.BlockSpec(memory_space=pltpu.VMEM)),
+        in_specs=[hbm, hbm],
+        out_specs=(vmem, vmem, vmem, vmem),
         scratch_shapes=[
-            pltpu.VMEM((PIXELS, BANDS), BF16),
             pltpu.VMEM((PLANE, 8, 128), F32),
             pltpu.VMEM((PLANE, 8, 128), F32),
             pltpu.VMEM((8, 128), F32),
@@ -197,14 +202,14 @@
             pltpu.VMEM((SIDE, BANDS), BF16),
             pltpu.VMEM((SIDE, BANDS), BF16),
             pltpu.VMEM((HALO, BANDS), BF16),
-            pltpu.SemaphoreType.DMA,
+            pltpu.SemaphoreType.DMA((2,)),
             pltpu.SemaphoreType.DMA((3,)),
             pltpu.SemaphoreType.DMA((3,)),
             pltpu.SemaphoreType.DMA((8,)),
             pltpu.SemaphoreType.DMA((8,)),
         ],
-        compiler_params=pltpu.CompilerParams(collective_id=0, has_side_effects=True),
-    )(cube)
+        compiler_params=pltpu.CompilerParams(collective_id=0, has_side_effects=True, vmem_limit_bytes=12 << 20),
+    )(cube, first)
 
 
 def split(values):
@@ -271,14 +276,10 @@
 
 
 def smooth_kernel(
-    gram_ref, halo_hbm, cube_hbm, start_ref, out_ref, proj_ref, u0, u1, u2, flow, halo_ref, cube_ref, sems
+    gram_ref, halo_ref, cube_ref, start_ref, out_hbm, proj_hbm, u0, u1, u2, flow, out_ref, proj_ref, sems
 ):
     wide = lax.axis_index("wide")
     narrow = lax.axis_index("narrow")
-    load_cube = pltpu.make_async_copy(cube_hbm, cube_ref, sems.at[0])
-    load_halo = pltpu.make_async_copy(halo_hbm, halo_ref, sems.at[1])
-    load_cube.start()
-    load_halo.start()
     basis = subspace(gram_ref[...], start_ref[...])
     low = basis.astype(BF16).astype(F32)
     fit = 4.0 * lax.dot_general(low, basis, TN, precision=HIGHEST, preferred_element_type=F32)
@@ -298,8 +299,8 @@
             for r in range(rows):
                 u0[half, row + r, col : col + count, :] = part[r * count : (r + 1) * count]
 
-    load_cube.wait()
-    load_halo.wait()
+    proj_copy = pltpu.make_async_copy(proj_ref, proj_hbm, sems.at[4])
+    proj_copy.start()
 
     @pl.loop(0, TILE_ROWS // 8)
     def _(index):
@@ -372,13 +373,24 @@
                         stages[turn + 1][half, row, first : first + count, :] = value
             return tuple(above)
 
-        start = tuple(flows(half, turn, first, count)[1] for half in range(2))
-        lax.fori_loop(0, (EXT_ROWS - 2 - 2 * turn) // 2, pair, start)
+        above = tuple(flows(half, turn, first, count)[1] for half in range(2))
+        if not final:
+            lax.fori_loop(0, (EXT_ROWS - 2 - 2 * turn) // 2, pair, above)
+            continue
+        copies = []
+        for part in range(4):
+            above = lax.fori_loop(part * 4, part * 4 + 4, pair, above)
+            rows = pl.ds(part * (PIXELS // 4), PIXELS // 4)
+            copy = pltpu.make_async_copy(out_ref.at[rows], out_hbm.at[rows], sems.at[part])
+            copy.start()
+            copies.append(copy)
+        for copy in copies + [proj_copy]:
+            copy.wait()
 
 
 def smooth(gram, halo, cube, start):
     vmem = pl.BlockSpec(memory_space=pltpu.VMEM)
-    hbm = pl.BlockSpec(memory_space=pl.ANY)
+    hbm = pl.BlockSpec(memory_space=pltpu.HBM)
     field = pltpu.VMEM((2, EXT_ROWS, EXT_COLS + 8, 128), F32)
     return pl.pallas_call(
         smooth_kernel,
@@ -386,15 +398,16 @@
             jax.ShapeDtypeStruct((PIXELS, BANDS), BF16),
             jax.ShapeDtypeStruct((BANDS, BANDS), F32),
         ),
-        in_specs=[vmem, hbm, hbm, vmem],
-        out_specs=(vmem, vmem),
+        in_specs=[vmem] * 4,
+        out_specs=(hbm, hbm),
         scratch_shapes=[
             field, field, field,
             pltpu.VMEM((2, 2, EXT_COLS + 16, 128), F32),
-            pltpu.VMEM((HALO, BANDS), BF16),
             pltpu.VMEM((PIXELS, BANDS), BF16),
-            pltpu.SemaphoreType.DMA((2,)),
+            pltpu.VMEM((BANDS, BANDS), F32),
+            pltpu.SemaphoreType.DMA((5,)),
         ],
+        compiler_params=pltpu.CompilerParams(vmem_limit_bytes=24 << 20),
     )(gram, halo, cube, start)
 
 
@@ -407,8 +420,9 @@
 
 def body(cube):
     flat = cube.reshape(PIXELS, BANDS)
-    gram, halo = exchange(flat)
-    restored, projector = smooth(gram, halo, flat, jnp.asarray(first_basis()))
+    flat = pltpu.with_memory_space_constraint(flat, pltpu.HBM)
+    first = pltpu.with_memory_space_constraint(jnp.asarray(first_basis()), pltpu.HBM)
+    restored, projector = smooth(*exchange(flat, first))
     return restored.reshape(TILE_ROWS, TILE_COLS, BANDS), projector
 
 

time: 40 us -> 35.5 us (0.89)
  Pallas kernels: 39.2 us -> 34.8 us
    pallas_call x1, Pallas kernels: 28.4 us -> 25.3 us  [exchange(): pl.pallas_call(exchange_kernel, out_shape=(jax.ShapeDtypeStruct((256, 128...]
    pallas_call x1, Pallas kernels: 10.8 us -> 9.47 us  [smooth(): pl.pallas_call(smooth_kernel, out_shape=(jax.ShapeDtypeStruct((PIXELS, BA...]
where the time goes in v3:
time: 35.5 us; the launch traced here: 35.4 us
  Pallas kernels  34.8 us (98%)
  between operations  0.64 us (2%)
    pallas_call x1, Pallas kernels, exchange(): pl.pallas_call(exchange_kernel, out_shape=(jax.ShapeDtypeStruct((256, 128...  25.3 us
    pallas_call x1, Pallas kernels, smooth(): pl.pallas_call(smooth_kernel, out_shape=(jax.ShapeDtypeStruct((PIXELS, BA...  9.47 us

profile of v3, /device:TPU:1, one launch (start us, length us, event | category | flops | bytes accessed | tf_op | source)
XLA Modules:
  0.0 35.4 jit_solution(18020654300355545499)
XLA Ops:
  0.6 25.3 %shard_map.41 = (f32[256,128]{1,0:T(8,128)S(1)}, bf16[608,224]{1,0:T(8,128)(2,1)S(1)}, bf16[1536,224]{1,0:T(8,128)(2,1)S(1)}, f32[16,256]{1,0:T(8,128)S(1)}) custom-call(bf16[1536,224]{1,0:T(8,128)(2,1)} %bitcast.2, f32[16,256]{1,0:T(8,128)} %constant.2.clone.first_ref), custom_call_target="tpu_custom_call" | custom-call | tf_op jit(solution)/shard_map/pallas_call | solution.py:186
  26.0 9.5 %shard_map.42 = (bf16[1536,224]{1,0:T(8,128)(2,1)}, f32[224,224]{1,0:T(8,128)}) custom-call(f32[256,128]{1,0:T(8,128)S(1)} %get-tuple-element.8.gram_ref, bf16[608,224]{1,0:T(8,128)(2,1)S(1)} %get-tuple-element.9.halo_ref, bf16[1536,224]{1,0:T(8,128)(2,1)S(1)} %get-tuple-element.10.cube_ref, f32[16,256]{1,0:T(8,128)S(1)} %get-tuple-element.11.start_ref), custom_call_target="tpu_custom_call" | custom-call | tf_op jit(solution)/shard_map/pallas_call | solution.py:395

commit v4 on v3

--- a/solution.py
+++ b/solution.py
@@ -236,20 +236,35 @@
 
 
 def orthonormal(inner, grown):
-    row = lax.broadcasted_iota(jnp.int32, (RANK, 128), 0)
-    cols = [jnp.broadcast_to(inner[:, k : k + 1], (RANK, 128)) for k in range(RANK)]
-    halves = [grown[:, :128], grown[:, 128:]]
-    pivots = jnp.zeros((RANK, 128), F32)
+    row = lax.broadcasted_iota(jnp.int32, (8, 128), 0)
+
+    def spread(k, half):
+        return jnp.broadcast_to(inner[8 * half : 8 * half + 8, k : k + 1], (8, 128))
+
+    cols = [[spread(k, 0) if k < 8 else None, spread(k, 1)] for k in range(RANK)]
+    rows = [[grown[8 * half : 8 * half + 8, at : at + 128] for at in (0, 128)] for half in range(2)]
+    pivots = [jnp.zeros((8, 128), F32)] * 2
     for step in range(RANK):
-        pivot = cols[step][step : step + 1]
-        pivots = jnp.where(row == step, pivot, pivots)
-        if step < RANK - 1:
-            factor = jnp.where(row > step, cols[step] * (1.0 / pivot), 0.0)
-            for k in range(step + 1, RANK):
-                cols[k] = cols[k] - factor * cols[k][step : step + 1]
-            halves = [half - factor * half[step : step + 1] for half in halves]
-    scale = lax.rsqrt(pivots)
-    return jnp.concatenate([half * scale for half in halves], axis=1)
+        own, local = step // 8, step % 8
+        column = cols[step]
+        pivot = column[own][local : local + 1]
+        pivots[own] = jnp.where(row == local, pivot, pivots[own])
+        if step == RANK - 1:
+            break
+        inverse = 1.0 / pivot
+        factor = [None, None]
+        for half in range(own, 2):
+            factor[half] = column[half] * inverse
+        factor[own] = jnp.where(row > local, factor[own], 0.0)
+        for k in range(step + 1, RANK):
+            value = column[k // 8][k % 8 : k % 8 + 1]
+            for half in range(k // 8, 2):
+                cols[k][half] = cols[k][half] - factor[half] * value
+        lead = [values[local : local + 1] for values in rows[own]]
+        for half in range(own, 2):
+            rows[half] = [values - factor[half] * top for values, top in zip(rows[half], lead)]
+    scaled = [[values * lax.rsqrt(pivots[half]) for values in rows[half]] for half in range(2)]
+    return jnp.concatenate([jnp.concatenate(part, axis=1) for part in scaled], axis=0)
 
 
 def subspace(packed, start):
@@ -281,12 +296,16 @@
     wide = lax.axis_index("wide")
     narrow = lax.axis_index("narrow")
     basis = subspace(gram_ref[...], start_ref[...])
-    low = basis.astype(BF16).astype(F32)
-    fit = 4.0 * lax.dot_general(low, basis, TN, precision=HIGHEST, preferred_element_type=F32)
-    high, rest, _ = split(fit[:BANDS])
-    proj_ref[...] = lax.dot_general(
-        basis, basis, TN, precision=HIGHEST, preferred_element_type=F32
-    )[:BANDS, :BANDS]
+    first, second, third = split(basis)
+
+    def outer(left, right):
+        return lax.dot_general(
+            jnp.concatenate(left, axis=0), jnp.concatenate(right, axis=0), TN, preferred_element_type=F32
+        )
+
+    fit = outer([first] * 3, [third, second, first])
+    high, rest, _ = split(4.0 * fit[:BANDS])
+    proj_ref[...] = (fit + outer([third, second, second], [first, second, first]))[:BANDS, :BANDS]
 
     def fitted(pixels):
         return jnp.dot(pixels, high, preferred_element_type=F32) + jnp.dot(
@@ -302,11 +321,7 @@
     proj_copy = pltpu.make_async_copy(proj_ref, proj_hbm, sems.at[4])
     proj_copy.start()
 
-    @pl.loop(0, TILE_ROWS // 8)
-    def _(index):
-        at = pl.multiple_of(index * (8 * TILE_COLS), 8 * TILE_COLS)
-        put(fitted(cube_ref[pl.ds(at, 8 * TILE_COLS), :]), 8, DEPTH + index * 8, 8, TILE_COLS)
-
+    put(fitted(cube_ref[...]), TILE_ROWS, DEPTH, 8, TILE_COLS)
     borders = fitted(halo_ref[...])
     put(borders[TOP : TOP + BORDER], DEPTH, 0, 8, TILE_COLS)
     put(borders[BOTTOM : BOTTOM + BORDER], DEPTH, DEPTH + TILE_ROWS, 8, TILE_COLS)
@@ -348,10 +363,12 @@
             scale = lax.rsqrt(gx * gx + gy * gy + 4.0)
             return middle, gx * scale, gy * scale
 
-        def pair(index, above):
+        unroll = (4, 4, 4)[turn]
+
+        def lines(index, above, count_rows, base):
             above = list(above)
-            for lane in range(2):
-                row = turn + 1 + 2 * index + lane
+            for lane in range(count_rows):
+                row = base + count_rows * index + lane
                 for half in range(2):
                     middle, px, py = flows(half, row, first, count)
                     flow[lane, half, 8 : 8 + count, :] = py
@@ -375,11 +392,16 @@
 
         above = tuple(flows(half, turn, first, count)[1] for half in range(2))
         if not final:
-            lax.fori_loop(0, (EXT_ROWS - 2 - 2 * turn) // 2, pair, above)
+            rows = EXT_ROWS - 2 - 2 * turn
+            steps = rows // unroll
+            above = lax.fori_loop(0, steps, lambda i, c: lines(i, c, unroll, turn + 1), above)
+            if rows % unroll:
+                lines(0, above, rows % unroll, turn + 1 + steps * unroll)
             continue
         copies = []
         for part in range(4):
-            above = lax.fori_loop(part * 4, part * 4 + 4, pair, above)
+            base = DEPTH + 8 * part
+            above = lax.fori_loop(0, 8 // unroll, lambda i, c, base=base: lines(i, c, unroll, base), above)
             rows = pl.ds(part * (PIXELS // 4), PIXELS // 4)
             copy = pltpu.make_async_copy(out_ref.at[rows], out_hbm.at[rows], sems.at[part])
             copy.start()
@@ -402,7 +424,7 @@
         out_specs=(hbm, hbm),
         scratch_shapes=[
             field, field, field,
-            pltpu.VMEM((2, 2, EXT_COLS + 16, 128), F32),
+            pltpu.VMEM((8, 2, EXT_COLS + 16, 128), F32),
             pltpu.VMEM((PIXELS, BANDS), BF16),
             pltpu.VMEM((BANDS, BANDS), F32),
             pltpu.SemaphoreType.DMA((5,)),

time: 35.5 us -> 34.1 us (0.961)
  Pallas kernels: 34.8 us -> 33.4 us
    pallas_call x1, Pallas kernels: 9.47 us -> 8.05 us  [smooth(): pl.pallas_call(smooth_kernel, out_shape=(jax.ShapeDtypeStruct((PIXELS, BA...]
where the time goes in v4:
time: 34.1 us; the launch traced here: 34 us
  Pallas kernels  33.4 us (98%)
  between operations  0.64 us (2%)
    pallas_call x1, Pallas kernels, exchange(): pl.pallas_call(exchange_kernel, out_shape=(jax.ShapeDtypeStruct((256, 128...  25.3 us
    pallas_call x1, Pallas kernels, smooth(): pl.pallas_call(smooth_kernel, out_shape=(jax.ShapeDtypeStruct((PIXELS, BA...  8.05 us

profile of v4, /device:TPU:1, one launch (start us, length us, event | category | flops | bytes accessed | tf_op | source)
XLA Modules:
  0.0 34.0 jit_solution(7353796518754462249)
XLA Ops:
  0.6 25.3 %shard_map.41 = (f32[256,128]{1,0:T(8,128)S(1)}, bf16[608,224]{1,0:T(8,128)(2,1)S(1)}, bf16[1536,224]{1,0:T(8,128)(2,1)S(1)}, f32[16,256]{1,0:T(8,128)S(1)}) custom-call(bf16[1536,224]{1,0:T(8,128)(2,1)} %bitcast.2, f32[16,256]{1,0:T(8,128)} %constant.2.clone.first_ref), custom_call_target="tpu_custom_call" | custom-call | tf_op jit(solution)/shard_map/pallas_call | solution.py:186
  26.0 8.1 %shard_map.42 = (bf16[1536,224]{1,0:T(8,128)(2,1)}, f32[224,224]{1,0:T(8,128)}) custom-call(f32[256,128]{1,0:T(8,128)S(1)} %get-tuple-element.8.gram_ref, bf16[608,224]{1,0:T(8,128)(2,1)S(1)} %get-tuple-element.9.halo_ref, bf16[1536,224]{1,0:T(8,128)(2,1)S(1)} %get-tuple-element.10.cube_ref, f32[16,256]{1,0:T(8,128)S(1)} %get-tuple-element.11.start_ref), custom_call_target="tpu_custom_call" | custom-call | tf_op jit(solution)/shard_map/pallas_call | solution.py:417
